TPU v7x, 128 devices: a whole 4x4x4 slice. The times are simulated.
128 devices in a mesh: tok: 16 (over x, z), head: 8 (over y, core).
Axes of the slice: x: 4, y: 4, z: 4, core: 2. Of those that a mesh axis runs over, the one named last changes fastest.
Arguments:
- tokens: bfloat16 [4096, 2880], P(('tok', 'head')), may hold values from -6 to 6
- lengths: int32 [4], replicated, may hold values from 1 to 2048, 3968 in all
- norm_gain_attn: float32 [2880], replicated, may hold values from 0.1 to 1.9
- query_key_value_weight: bfloat16 [2880, 5120], P(None, 'head'), may hold values from -0.109375 to 0.109375
- sinks: float32 [64], P('head'), may hold values from 1 to 6
- w_out_attn: bfloat16 [4096, 2880], P('head'), may hold values from -0.09375 to 0.09375
- norm_gain_moe: float32 [2880], replicated, may hold values from 0.1 to 1.9
- routes: int32 [4096, 4], P(('tok', 'head')), may hold values from 0 to 31, all different within a row; in each aligned block of 32 rows (0 to 31, 32 to 63, ...) at most 6 rows name the same one
- gates: float32 [4096, 4], P(('tok', 'head')), may hold values from 0.1 to 1
- w_in: bfloat16 [128, 2880, 1440], P(('tok', 'head')), may hold values from -0.109375 to 0.109375
- w_down: bfloat16 [128, 720, 2880], P(('tok', 'head')), may hold values from -0.109375 to 0.109375
- page_table: int32 [256], replicated, may hold values from 0 to 255, as said below
Outputs:
- hidden_out: bfloat16 [4096, 2880], P(('tok', 'head'))
- kv_cache: bfloat16 [8, 256, 16, 128], P('head', 'tok')
Inputs may be any that keep to these rules, and one draw needn't show every extreme that they name: `routes`: every row names 4 different experts. In each aligned block of 32 rows no expert is named by more than 6 rows, and in every draw some block has an expert named by exactly 6 rows. `lengths`: they sum to 3968, and the longest is exactly 2048. `page_table`: A permutation. Of the 16 logical pages in each aligned block of 16, exactly 1 map into each aligned block of 16 physical pages.
All inputs are finite; a program needn't handle non-finite values.
Results may differ from a plain program's by a relative error of at most 0.018.
Values may be sent and summed in bfloat16 or wider, within the bound.
A program may use at most 128 MiB of HBM per device.

v0:
```python
import math
import jax
import jax.numpy as jnp
from jax import lax
from jax.sharding import PartitionSpec as P

MODEL_WIDTH = 2880
HEAD_SIZE = 64
EXPERTS = 32
ATTEND_WINDOW = 128
NSEQ = 4
PAGE_TOKENS = 16
QUERY_PER_KEY = 8
EPSILON = 1e-05
ROPE_BASE = 150000.0
GLU_ALPHA = 1.702


def passed_along(array, axis, by):
    peers = lax.axis_size(axis)
    pairs = [(i, i + by) for i in range(peers) if 0 <= i + by < peers]
    return lax.ppermute(array, axis, pairs)


def normalize(values, gain_vec):
    wide = values.astype(jnp.float32)
    inv_rms = lax.rsqrt(jnp.mean(wide * wide, axis=-1, keepdims=True) + EPSILON)
    return wide * inv_rms * gain_vec


def segment_table(lengths, row_index):
    seq_ends = jnp.cumsum(lengths)
    starts = jnp.concatenate([jnp.zeros((1,), jnp.int32), seq_ends])
    segment = jnp.sum((row_index[:, None] >= seq_ends[None, :]).astype(jnp.int32), axis=1)
    onehot = segment[:, None] == jnp.arange(starts.shape[0], dtype=jnp.int32)[None, :]
    seg_start = jnp.sum(jnp.where(onehot, starts[None, :], 0), axis=1)
    return (segment, row_index - seg_start)


def rotate(values, positions):
    half_dim = values.shape[-1] // 2
    inv_freq = jnp.exp(
        jnp.arange(half_dim, dtype=jnp.float32) * (-2.0 * math.log(ROPE_BASE) / values.shape[-1])
    )
    angles = positions.astype(jnp.float32)[:, None] * inv_freq[None, :]
    view_shape = (angles.shape[0],) + (1,) * (values.ndim - 2) + (half_dim,)
    cos_table = jnp.cos(angles).reshape(view_shape)
    sin_table = jnp.sin(angles).reshape(view_shape)
    lower_half = values[..., :half_dim]
    upper_half = values[..., half_dim:]
    return jnp.concatenate(
        [
            lower_half * cos_table - upper_half * sin_table,
            upper_half * cos_table + lower_half * sin_table,
        ],
        axis=-1,
    )


def band_mask(query_index, key_index, query_segs, key_segs, window):
    nblocks = query_index.shape[0] // window
    query_pos = query_index.reshape(nblocks, window)
    query_seg = query_segs.reshape(nblocks, window)
    key_grid = key_index.reshape(nblocks + 1, window)
    seg_grid = key_segs.reshape(nblocks + 1, window)
    key_pos = jnp.concatenate([key_grid[:-1], key_grid[1:]], axis=1)
    key_seg = jnp.concatenate([seg_grid[:-1], seg_grid[1:]], axis=1)
    distance = query_pos[:, :, None] - key_pos[:, None, :]
    allowed = (query_seg[:, :, None] == key_seg[:, None, :]) & (query_seg < NSEQ)[:, :, None]
    allowed = allowed & (key_pos >= 0)[:, None, :] & (distance >= 0) & (distance < window)
    return allowed


def band_attention(query_rows, extended, sink_table, allowed):
    nblocks = allowed.shape[0]
    groups = sink_table.shape[0]
    query_blocks = query_rows.reshape(nblocks, ATTEND_WINDOW, groups, QUERY_PER_KEY, HEAD_SIZE)
    pair_grid = extended.reshape(nblocks + 1, ATTEND_WINDOW, groups, 2 * HEAD_SIZE)
    key_band = jnp.concatenate([pair_grid[:-1], pair_grid[1:]], axis=1)
    scores = jnp.einsum(
        "bqgnh,bkgh->bgnqk",
        query_blocks,
        key_band[..., :HEAD_SIZE],
        preferred_element_type=jnp.float32,
    )
    weights = jnp.where(allowed[:, None, None], jnp.exp(scores), 0.0)
    totals = jnp.sum(weights, axis=-1, keepdims=True) + jnp.exp(sink_table)[None, :, :, None, None]
    probs_bf = (weights / totals).astype(jnp.bfloat16)
    outputs = jnp.einsum(
        "bgnqk,bkgh->bqgnh", probs_bf, key_band[..., HEAD_SIZE:], preferred_element_type=jnp.float32
    )
    return outputs.astype(jnp.bfloat16).reshape(
        nblocks * ATTEND_WINDOW, groups * QUERY_PER_KEY * HEAD_SIZE
    )


def expert_mlp(rows_in, w_in_local, w_down_local):
    ffs_local = w_down_local.shape[0]
    gate_up = jnp.dot(rows_in, w_in_local, preferred_element_type=jnp.float32)
    gate_part = gate_up[:, :ffs_local]
    up_part = gate_up[:, ffs_local:]
    activated = ((up_part + 1.0) * gate_part * jax.nn.sigmoid(GLU_ALPHA * gate_part)).astype(
        jnp.bfloat16
    )
    return jnp.dot(activated, w_down_local, preferred_element_type=jnp.float32).astype(jnp.bfloat16)


def copied_route(outgoing, route, width_split, slots, w_in_local, w_down_local):
    spread = jnp.broadcast_to(
        outgoing[:, None], (EXPERTS, width_split, slots, MODEL_WIDTH)
    ).reshape(EXPERTS * width_split, slots, MODEL_WIDTH)
    incoming = route(spread)
    produced = expert_mlp(incoming.reshape(-1, MODEL_WIDTH), w_in_local, w_down_local).reshape(
        spread.shape
    )
    returned = route(produced)
    return jnp.sum(
        returned.astype(jnp.float32).reshape(EXPERTS, width_split, slots, MODEL_WIDTH), axis=1
    ).reshape(EXPERTS * slots, MODEL_WIDTH)


def page_order(page_table, n_tok, pages_dev):
    page_grid = page_table.reshape(n_tok, pages_dev)
    target = page_grid // pages_dev
    page_ids = jnp.arange(pages_dev, dtype=jnp.int32)
    earlier = page_ids[:, None] > page_ids[None, :]
    same_dest = target[:, :, None] == target[:, None, :]
    order_rank = jnp.sum((same_dest & earlier[None]).astype(jnp.int32), axis=2)
    return (target, order_rank, page_grid % pages_dev)


def per_device(
    tokens,
    lengths,
    norm_gain_attn,
    query_key_value_weight,
    sinks,
    w_out_attn,
    norm_gain_moe,
    routes,
    gates,
    w_in,
    w_down,
    page_table,
):
    n_tok = lax.axis_size("tok")
    n_head = lax.axis_size("head")
    tok_id = lax.axis_index("tok")
    head_id = lax.axis_index("head")
    row_count = tokens.shape[0]
    tok_dev = row_count * n_head
    groups = sinks.shape[0] // QUERY_PER_KEY
    normed_input = normalize(tokens, norm_gain_attn).astype(jnp.bfloat16)
    projected_rows = jnp.dot(
        lax.all_gather(normed_input, "head", axis=0, tiled=True),
        query_key_value_weight,
        preferred_element_type=jnp.float32,
    ).reshape(tok_dev, groups, QUERY_PER_KEY + 2, HEAD_SIZE)
    row_base = tok_id * tok_dev
    query_index = row_base + jnp.arange(tok_dev, dtype=jnp.int32)
    query_segs, positions = segment_table(lengths, query_index)
    query_rows = (
        rotate(projected_rows[:, :, :QUERY_PER_KEY], positions) * HEAD_SIZE ** (-0.5)
    ).astype(jnp.bfloat16)
    key_rot = rotate(projected_rows[:, :, QUERY_PER_KEY], positions)
    key_value_pairs = jnp.concatenate(
        [key_rot, projected_rows[:, :, QUERY_PER_KEY + 1]], axis=-1
    ).astype(jnp.bfloat16)
    rim_rows = passed_along(key_value_pairs[tok_dev - ATTEND_WINDOW :], "tok", 1)
    key_index = row_base - ATTEND_WINDOW + jnp.arange(tok_dev + ATTEND_WINDOW, dtype=jnp.int32)
    key_segs, _ = segment_table(lengths, key_index)
    allowed = band_mask(query_index, key_index, query_segs, key_segs, ATTEND_WINDOW)
    attended = band_attention(
        query_rows,
        jnp.concatenate([rim_rows, key_value_pairs], axis=0),
        sinks.reshape(groups, QUERY_PER_KEY),
        allowed,
    )
    attn_sum = lax.psum_scatter(
        jnp.dot(attended, w_out_attn, preferred_element_type=jnp.float32).astype(jnp.bfloat16),
        "head",
        scatter_dimension=0,
        tiled=True,
    ).astype(jnp.float32)
    resid = tokens.astype(jnp.float32) + attn_sum
    moe_in = normalize(resid, norm_gain_moe).astype(jnp.bfloat16)
    own_index = row_base + head_id * row_count + jnp.arange(row_count, dtype=jnp.int32)
    own_segs, _ = segment_table(lengths, own_index)
    is_live = own_segs < NSEQ
    capacity = row_count // 8 + 2
    width_split = n_tok * n_head // EXPERTS
    expert_ids = jnp.arange(EXPERTS, dtype=jnp.int32)
    naming = routes[:, :, None] == expert_ids[None, None, :]
    routed = (jnp.any(naming, axis=1) & is_live[:, None]).astype(jnp.int32)
    slot_rank = jnp.cumsum(routed, axis=0) - 1
    slot_ids = jnp.arange(capacity, dtype=jnp.int32)
    placed = (routed == 1)[:, :, None] & (slot_rank[:, :, None] == slot_ids[None, None, :])
    local_ids = jnp.arange(row_count, dtype=jnp.int32)
    source_row = jnp.sum(jnp.where(placed, local_ids[:, None, None], 0), axis=0)
    filled = jnp.any(placed, axis=0)
    outgoing = jnp.where(filled[:, :, None], moe_in[source_row], jnp.zeros((), jnp.bfloat16))

    def flat_route(blocks):
        return lax.all_to_all(blocks, ("tok", "head"), split_axis=0, concat_axis=0, tiled=True)

    summed = copied_route(outgoing, flat_route, width_split, capacity, w_in[0], w_down[0])
    chosen_rank = jnp.sum(jnp.where(naming, slot_rank[:, None, :], 0), axis=2)
    pick_rows = routes * capacity + jnp.clip(chosen_rank, 0, capacity - 1)
    weighted = jnp.where(is_live[:, None], gates, 0.0)
    expert_sum = jnp.sum(summed[pick_rows] * weighted[:, :, None], axis=1)
    hidden_out = (resid + expert_sum).astype(jnp.bfloat16)
    pages_dev = tok_dev // PAGE_TOKENS
    share_count = pages_dev // n_tok
    paged = key_value_pairs.reshape(pages_dev, PAGE_TOKENS, groups, 2 * HEAD_SIZE)
    target, order_rank, slot_grid = page_order(page_table, n_tok, pages_dev)
    dest_ids = jnp.arange(n_tok, dtype=jnp.int32)
    share_ids = jnp.arange(share_count, dtype=jnp.int32)
    page_ids = jnp.arange(pages_dev, dtype=jnp.int32)
    my_target = target[tok_id]
    my_rank = order_rank[tok_id]
    matched = (my_target[:, None, None] == dest_ids[None, :, None]) & (
        my_rank[:, None, None] == share_ids[None, None, :]
    )
    pick_page = jnp.sum(jnp.where(matched, page_ids[:, None, None], 0), axis=0)
    arrived = lax.all_to_all(paged[pick_page], "tok", split_axis=0, concat_axis=0, tiled=True)
    to_here = (target == tok_id)[:, :, None] & (order_rank[:, :, None] == share_ids[None, None, :])
    landing = jnp.sum(jnp.where(to_here, slot_grid[:, :, None], 0), axis=1)
    stored = jnp.zeros_like(paged).at[landing.reshape(-1)].set(arrived.reshape(paged.shape))
    kv_cache = jnp.transpose(stored, (2, 0, 1, 3))
    return (hidden_out, kv_cache)


def solution(mesh):
    return jax.shard_map(
        per_device,
        mesh=mesh,
        in_specs=(
            P(("tok", "head"), None),
            P(),
            P(),
            P(None, "head"),
            P("head"),
            P("head", None),
            P(),
            P(("tok", "head"), None),
            P(("tok", "head"), None),
            P(("tok", "head"), None, None),
            P(("tok", "head"), None, None),
            P(),
        ),
        out_specs=(P(("tok", "head"), None), P("head", "tok", None, None)),
        check_vma=False,
    )
```

profile of v0, /device:TPU:0, one launch (start us, length us, event | category | flops | bytes accessed | tf_op | source)
XLA Modules:
  0.0 337.7 jit_solution(5325949729311232361)
XLA Ops:
  8.5 1.7 fusion.15
  14.6 22.5 %all-gather.2.cloned.1.call-done = bf16[256,2880]{1,0:T(8,128)(2,1)} async-done(((bf16[32,2880]{1,0:T(8,128)(2,1)}), bf16[256,2880]{1,0:T(8,128)(2,1)}) %all-gather.2.cloned.1.call-update) | async-done | bytes 1474576 | tf_op jit(solution)/shard_map/all_gather | solution.py:155
  37.1 4.1 %fusion.49 = f32[256,640]{0,1:T(8,128)S(1)} fusion(bf16[256,2880]{1,0:T(8,128)(2,1)} %all-gather.2.cloned.1.call-done, bf16[2880,640]{1,0:T(8,128)(2,1)} %param.15), kind=kOutput, calls=%fused_computation.145 | convolution fusion | flops 943718400 | bytes 5816320 | tf_op jit(solution)/shard_map/dot_general | solution.py:154
  42.0 4.1 %collective-permute-start = (bf16[128,1,128]{0,2,1:T(8,128)(2,1)}, bf16[128,1,128]{0,2,1:T(8,128)(2,1)}, u32[]{:S(2)}, u32[]{:S(2)}) collective-permute-start(bf16[128,1,128]{0,2,1:T(8,128)(2,1)} %pad_maximum_fusion.3), channel_id=1, source_target_pairs={{0,8},{8,16},{16,24},{24,32},{32,40},{40,48},{48,56},{56,64},{64,7... | collective-permute-start | bytes 98312 | tf_op jit(solution)/shard_map/ppermute | solution.py:22
  51.0 1.7 copy.77
  57.1 2.2 convolution_convert_fusion.1
  60.1 31.5 %reduce-scatter.2.cloned.1.call-done = bf16[32,2880]{1,0:T(8,128)(2,1)} async-done(((bf16[256,2880]{1,0:T(8,128)(2,1)}), bf16[32,2880]{1,0:T(8,128)(2,1)}) %reduce-scatter.2.cloned.1.call-update) | async-done | bytes 184336 | tf_op jit(solution)/shard_map/reduce_scatter | solution.py:179
  96.5 1.6 broadcast_select_fusion
  98.1 3.0 broadcast_in_dim.93
  101.1 8.1 %all-to-all-start = ((bf16[128,6,2880]{2,1,0:T(8,128)(2,1)}), bf16[128,6,2880]{2,1,0:T(8,128)(2,1)}, u32[]{:S(2)}, u32[]{:S(2)}) async-start(bf16[128,6,2880]{2,1,0:T(8,128)(2,1)} %bitcast.119), calls=%async_computation.1 | async-start | bytes 12058624 | tf_op jit(solution)/shard_map/all_to_all | solution.py:204
  111.6 70.6 %all-to-all-done = bf16[128,6,2880]{2,1,0:T(8,128)(2,1)} async-done(((bf16[128,6,2880]{2,1,0:T(8,128)(2,1)}), bf16[128,6,2880]{2,1,0:T(8,128)(2,1)}, u32[]{:S(2)}, u32[]{:S(2)}) %all-to-all-start) | async-done | bytes 4423712 | tf_op jit(solution)/shard_map/all_to_all | solution.py:204
  182.2 6.4 %all-to-all-start.2 = ((bf16[16,1,16,1,128]{4,2,3,1,0:T(8,128)(2,1)}), bf16[16,1,16,1,128]{4,2,3,1,0:T(8,128)(2,1)S(1)}, u32[]{:S(2)}, u32[]{:S(2)}) async-start(bf16[16,1,16,1,128]{4,2,3,1,0:T(8,128)(2,1)} %bitcast.37), calls=%async_computation.3 | async-start | bytes 131072 | tf_op jit(solution)/shard_map/all_to_all | solution.py:225
  188.6 8.2 %reshape.821 = bf16[768,2880]{1,0:T(8,128)(2,1)} reshape(bf16[128,6,2880]{2,1,0:T(8,128)(2,1)} %all-to-all-done) | data formatting | bytes 8847360 | tf_op jit(solution)/shard_map/reshape | solution.py:113
  196.8 10.8 %fusion = f32[768,1440]{0,1:T(8,128)S(1)} fusion(bf16[768,2880]{1,0:T(8,128)(2,1)} %reshape.821, bf16[1,2880,1440]{1,2,0:T(8,128)(2,1)} %param.21), kind=kOutput, calls=%fused_computation.5 | convolution fusion | flops 6370099200 | bytes 17141760 | tf_op jit(solution)/shard_map/dot_general | solution.py:99
  207.6 8.1 %convolution_convert_fusion = bf16[768,2880]{0,1:T(8,128)(2,1)} fusion(bf16[1,720,2880]{2,1,0:T(8,128)(2,1)} %param.22, f32[768,1440]{0,1:T(8,128)S(1)} %fusion), kind=kOutput, calls=%fused_computation.7 | convolution fusion | flops 3191685120 | bytes 12994560 | tf_op jit(solution)/shard_map/dot_general | solution.py:105
  215.7 6.5 %copy.83 = bf16[768,2880]{1,0:T(8,128)(2,1)} copy(bf16[768,2880]{0,1:T(8,128)(2,1)} %convolution_convert_fusion) | data formatting | bytes 8847360 | tf_op jit(solution)/shard_map/convert_element_type | solution.py:105
  222.2 7.6 %reshape.822 = bf16[128,6,2880]{2,1,0:T(8,128)(2,1)} reshape(bf16[768,2880]{1,0:T(8,128)(2,1)} %copy.83) | data formatting | bytes 8847360 | tf_op jit(solution)/shard_map/reshape | solution.py:113
  229.8 8.6 %all-to-all-start.1 = ((bf16[128,6,2880]{2,1,0:T(8,128)(2,1)}), bf16[128,6,2880]{2,1,0:T(8,128)(2,1)}, u32[]{:S(2)}, u32[]{:S(2)}) async-start(bf16[128,6,2880]{2,1,0:T(8,128)(2,1)} %reshape.822), calls=%async_computation.2 | async-start | bytes 12058624 | tf_op jit(solution)/shard_map/all_to_all | solution.py:204
  240.2 71.0 %all-to-all-done.1 = bf16[128,6,2880]{2,1,0:T(8,128)(2,1)} async-done(((bf16[128,6,2880]{2,1,0:T(8,128)(2,1)}), bf16[128,6,2880]{2,1,0:T(8,128)(2,1)}, u32[]{:S(2)}, u32[]{:S(2)}) %all-to-all-start.1) | async-done | bytes 4423712 | tf_op jit(solution)/shard_map/all_to_all | solution.py:204
  311.2 6.0 %convert_reduce_fusion = f32[32,6,2880]{2,1,0:T(8,128)} fusion(bf16[128,6,2880]{2,1,0:T(8,128)(2,1)} %all-to-all-done.1), kind=kLoop, calls=%fused_computation.4 | loop fusion | flops 3870720 | bytes 6635520 | tf_op jit(solution)/shard_map/reduce_sum | solution.py:117
  317.2 3.0 reshape.825
  320.2 4.6 %gather_fusion.1 = f32[128,2880]{1,0:T(8,128)} fusion(f32[192,2880]{1,0:T(8,128)} %reshape.825, s32[1024]{0:T(1024)S(1)} %pad_clamp_fusion.1), kind=kCustom, calls=%fused_computation.1 | custom fusion | bytes 2949632 | tf_op jit(solution)/shard_map/gather | solution.py:210
  324.9 2.8 reshape.840
  327.7 2.4 multiply_reduce_fusion
  (125 shorter events, 26.1 us)
Async XLA Ops:
  7.2 49.9 %copy-start = (bf16[512,2880]{0,1:T(8,128)(2,1)S(1)}, bf16[512,2880]{0,1:T(8,128)(2,1)}, u32[]{:S(2)}) copy-start(bf16[512,2880]{0,1:T(8,128)(2,1)} %param.17) | copy-start | bytes 8847364
  7.2 29.9 %all-gather.2.cloned.1.call-start = ((), (), s32[]{:S(2)}) async-start(), calls=%async_computation.4 | async-start | bytes 1695744 | tf_op jit(solution)/shard_map/all_gather | solution.py:155
  10.2 81.4 %reduce-scatter.2.cloned.1.call-start = ((), (), s32[]{:S(2)}) async-start(), calls=%async_computation.5 | async-start | bytes 1695744 | tf_op jit(solution)/shard_map/reduce_scatter | solution.py:179
  12.3 0.5 copy-start.12
  37.1 9.0 %copy-start.7 = (f32[256,32]{0,1:T(8,128)S(1)}, f32[256,32]{0,1:T(8,128)}, u32[]{:S(2)}) copy-start(f32[256,32]{0,1:T(8,128)} %get-tuple-element.12) | copy-start | bytes 98308
  37.1 9.0 %copy-start.8 = (f32[256,32]{0,1:T(8,128)S(1)}, f32[256,32]{0,1:T(8,128)}, u32[]{:S(2)}) copy-start(f32[256,32]{0,1:T(8,128)} %get-tuple-element.13) | copy-start | bytes 98308
  42.0 10.8 %collective-permute-start = (bf16[128,1,128]{0,2,1:T(8,128)(2,1)}, bf16[128,1,128]{0,2,1:T(8,128)(2,1)}, u32[]{:S(2)}, u32[]{:S(2)}) collective-permute-start(bf16[128,1,128]{0,2,1:T(8,128)(2,1)} %pad_maximum_fusion.3), channel_id=1, source_target_pairs={{0,8},{8,16},{16,24},{24,32},{32,40},{40,48},{48,56},{56,64},{64,7... | collective-permute-start | bytes 98312 | tf_op jit(solution)/shard_map/ppermute | solution.py:22
  52.8 3.4 %copy-start.5 = (pred[2,128,256]{1,2,0:T(8,128)(4,1)S(1)}, pred[2,128,256]{1,2,0:T(8,128)(4,1)}, u32[]{:S(2)}) copy-start(pred[2,128,256]{1,2,0:T(8,128)(4,1)} %fusion.22) | copy-start | bytes 196612
  53.6 2.5 copy-start.15
  57.0 2.3 copy-start.13
  57.1 2.4 copy-start.9
  57.1 34.5 %copy-start.2 = (bf16[32,2880]{1,0:T(8,128)(2,1)S(1)}, bf16[32,2880]{1,0:T(8,128)(2,1)}, u32[]{:S(2)}) copy-start(bf16[32,2880]{1,0:T(8,128)(2,1)} %param.12) | copy-start | bytes 552964
  57.1 35.6 %copy-start.10 = (f32[2880]{0:T(1024)S(1)}, f32[2880]{0:T(1024)}, u32[]{:S(2)}) copy-start(f32[2880]{0:T(1024)} %param.18) | copy-start | bytes 34564
  101.1 8.1 %copy-start.11 = (s32[256]{0:T(256)S(1)}, s32[256]{0:T(256)}, u32[]{:S(2)}) copy-start(s32[256]{0:T(256)} %param.23) | copy-start | bytes 3076
  101.1 9.0 %copy-start.4 = (bf16[256,1,1,64]{0,3,2,1:T(8,128)(2,1)S(1)}, bf16[256,1,1,64]{0,3,2,1:T(8,128)(2,1)}, u32[]{:S(2)}) copy-start(bf16[256,1,1,64]{0,3,2,1:T(8,128)(2,1)} %slice.143) | copy-start | bytes 98308
  101.1 81.1 %all-to-all-start = ((bf16[128,6,2880]{2,1,0:T(8,128)(2,1)}), bf16[128,6,2880]{2,1,0:T(8,128)(2,1)}, u32[]{:S(2)}, u32[]{:S(2)}) async-start(bf16[128,6,2880]{2,1,0:T(8,128)(2,1)} %bitcast.119), calls=%async_computation.1 | async-start | bytes 12058624 | tf_op jit(solution)/shard_map/all_to_all | solution.py:204
  182.2 47.6 %all-to-all-start.2 = ((bf16[16,1,16,1,128]{4,2,3,1,0:T(8,128)(2,1)}), bf16[16,1,16,1,128]{4,2,3,1,0:T(8,128)(2,1)S(1)}, u32[]{:S(2)}, u32[]{:S(2)}) async-start(bf16[16,1,16,1,128]{4,2,3,1,0:T(8,128)(2,1)} %bitcast.37), calls=%async_computation.3 | async-start | bytes 131072 | tf_op jit(solution)/shard_map/all_to_all | solution.py:225
  229.8 9.1 %copy-start.14 = (f32[32,4]{0,1:T(4,128)S(1)}, f32[32,4]{0,1:T(4,128)}, u32[]{:S(2)}) copy-start(f32[32,4]{0,1:T(4,128)} %param.20) | copy-start | bytes 1540
  229.8 81.4 %all-to-all-start.1 = ((bf16[128,6,2880]{2,1,0:T(8,128)(2,1)}), bf16[128,6,2880]{2,1,0:T(8,128)(2,1)}, u32[]{:S(2)}, u32[]{:S(2)}) async-start(bf16[128,6,2880]{2,1,0:T(8,128)(2,1)} %reshape.822), calls=%async_computation.2 | async-start | bytes 12058624 | tf_op jit(solution)/shard_map/all_to_all | solution.py:204
  240.2 77.0 %copy-start.6 = (bf16[16,16,128]{2,1,0:T(8,128)(2,1)}, bf16[16,16,128]{2,1,0:T(8,128)(2,1)S(1)}, u32[]{:S(2)}) copy-start(bf16[16,16,128]{2,1,0:T(8,128)(2,1)S(1)} %scatter_fusion) | copy-start | bytes 196612
  320.2 10.6 %copy-start.1 = (bf16[512,2880]{0,1:T(8,128)(2,1)S(1)}, bf16[512,2880]{0,1:T(8,128)(2,1)}, u32[]{:S(2)}) copy-start(bf16[512,2880]{0,1:T(8,128)(2,1)} %param.17) | copy-start | bytes 8847364
  324.9 5.2 %copy-start.3 = (bf16[32,2880]{1,0:T(8,128)(2,1)S(1)}, bf16[32,2880]{1,0:T(8,128)(2,1)}, u32[]{:S(2)}) copy-start(bf16[32,2880]{1,0:T(8,128)(2,1)} %reduce-scatter.2.cloned.1.call-done) | copy-start | bytes 552964
Sparse Core Ops, SparseCore 0:
  10.3 26.7 all-gather.1
  59.4 32.1 reduce-scatter.1
where the time goes:
time: 339 us; the launch traced here: 338 us
  waiting for transfers between devices  196 us (58%)
  local copies, waits for them, and re-layouts  50.4 us (15%)
  starting transfers between devices  27.2 us (8%)
  matrix products  27.2 us (8%)
  other arithmetic  22.7 us (7%)
  between operations  14.5 us (4%)
    all_to_all x2, waiting for transfers between devices, flat_route(): lax.all_to_all(blocks, ('tok', 'head'), split_axis=0, concat_axis=0, tile...  142 us
    reduce_scatter x1, waiting for transfers between devices, per_device(): lax.psum_scatter(jnp.dot(attended, w_out_attn, preferred_element_type=jnp...  31.5 us
    all_gather x1, waiting for transfers between devices, per_device(): lax.all_gather(normed_input, 'head', axis=0, tiled=True)  22.5 us
    all_to_all x2, starting transfers between devices, flat_route(): lax.all_to_all(blocks, ('tok', 'head'), split_axis=0, concat_axis=0, tile...  16.7 us
    dot_general x1, matrix products, expert_mlp(): gate_up = jnp.dot(rows_in, w_in_local, preferred_element_type=jnp.float32)  10.8 us
    reshape x1, local copies, waits for them, and re-layouts, copied_route(): incoming.reshape(-1, MODEL_WIDTH)  8.19 us
    dot_general x1, matrix products, expert_mlp(): jnp.dot(activated, w_down_local, preferred_element_type=jnp.float32)  8.09 us
    reshape x1, local copies, waits for them, and re-layouts, copied_route(): expert_mlp(incoming.reshape(-1, MODEL_WIDTH), w_in_local, w_down_local)  7.59 us
  transfers between devices with their start and end apart: 6, of which 4 were waited for; matrix products, arithmetic and copies ran while one was open for 17% of the time, Pallas kernels for 0%

commit v1 on v0

--- a/solution.py
+++ b/solution.py
@@ -1,3 +1,4 @@
+import functools
 import math
 import jax
 import jax.numpy as jnp
@@ -14,6 +15,33 @@
 EPSILON = 1e-05
 ROPE_BASE = 150000.0
 GLU_ALPHA = 1.702
+
+
+def plan_series_all_over_axis(frame, row_dim):
+    block_next = list(frame.shape[1:])
+    block_next[row_dim] *= frame.shape[0]
+    return jnp.moveaxis(frame, 0, row_dim).reshape(block_next)
+
+
+def detail_ratios(matrix, link_axis, at_axis):
+    workers = lax.axis_size(link_axis)
+    by_rank = [(kk, (kk + 1) % workers) for kk in range(workers)]
+    pages = [(src_i, dev) for dev, src_i in by_rank]
+    local_part, u1 = ([], [])
+    for tick in range(workers - 1):
+        if tick % 2 == 0:
+            local_part.append(
+                lax.ppermute(local_part[-1] if local_part else matrix, link_axis, perm=by_rank)
+            )
+        else:
+            u1.append(lax.ppermute(u1[-1] if u1 else matrix, axis_name=link_axis, perm=pages))
+    outcome_arr = jnp.stack([*local_part[::-1], matrix, *u1])
+    y2 = lax.axis_index(link_axis) - len(local_part)
+    outcome_arr = outcome_arr[(jnp.arange(workers) - y2) % workers]
+    return plan_series_all_over_axis(outcome_arr, at_axis)
+
+
+settle_panel = functools.partial(detail_ratios, link_axis="head", at_axis=0)
 
 
 def passed_along(array, axis, by):
@@ -152,9 +180,7 @@
     groups = sinks.shape[0] // QUERY_PER_KEY
     normed_input = normalize(tokens, norm_gain_attn).astype(jnp.bfloat16)
     projected_rows = jnp.dot(
-        lax.all_gather(normed_input, "head", axis=0, tiled=True),
-        query_key_value_weight,
-        preferred_element_type=jnp.float32,
+        settle_panel(normed_input), query_key_value_weight, preferred_element_type=jnp.float32
     ).reshape(tok_dev, groups, QUERY_PER_KEY + 2, HEAD_SIZE)
     row_base = tok_id * tok_dev
     query_index = row_base + jnp.arange(tok_dev, dtype=jnp.int32)

time: 339 us -> 348 us (1.027)
  waiting for transfers between devices: 196 us -> 183 us
  local copies, waits for them, and re-layouts: 50.4 us -> 60.6 us
  starting transfers between devices: 27.2 us -> 36.2 us
    all_gather x1 -> x0, waiting for transfers between devices: 22.5 us -> none  [per_device(): lax.all_gather(normed_input, 'head', axis=0, tiled=True)]
    unnamed x32 -> x45, local copies, waits for them, and re-layouts: 0.19 us -> 10.8 us
    ppermute x0 -> x7, waiting for transfers between devices: none -> 10.3 us  [the longest x4 10.3 us: detail_ratios(): lax.ppermute(local_part[-1] if local_part else matrix, link_axis, perm=by...]
    ppermute x0 -> x7, starting transfers between devices: none -> 8.89 us  [the longest x3 8.86 us: detail_ratios(): lax.ppermute(u1[-1] if u1 else matrix, axis_name=link_axis, perm=pages)]
  transfers between devices with their start and end apart: 6 -> 12, of which waited for: 4 -> 6; matrix products, arithmetic and copies ran while one was open for 17% -> 20% of each run, Pallas kernels for 0% -> 0%
where the time goes in v1:
time: 348 us; the launch traced here: 347 us
  waiting for transfers between devices  183 us (53%)
  local copies, waits for them, and re-layouts  60.6 us (17%)
  starting transfers between devices  36.2 us (10%)
  matrix products  26.9 us (8%)
  other arithmetic  25.5 us (7%)
  between operations  14.5 us (4%)
    all_to_all x2, waiting for transfers between devices, flat_route(): lax.all_to_all(blocks, ('tok', 'head'), split_axis=0, concat_axis=0, tile...  142 us
    reduce_scatter x1, waiting for transfers between devices, per_device(): lax.psum_scatter(jnp.dot(attended, w_out_attn, preferred_element_type=jnp...  30.9 us
    all_to_all x2, starting transfers between devices, flat_route(): lax.all_to_all(blocks, ('tok', 'head'), split_axis=0, concat_axis=0, tile...  16.4 us
    unnamed x45, local copies, waits for them, and re-layouts  10.8 us
    dot_general x1, matrix products, expert_mlp(): gate_up = jnp.dot(rows_in, w_in_local, preferred_element_type=jnp.float32)  10.8 us
    ppermute x4, waiting for transfers between devices, detail_ratios(): lax.ppermute(local_part[-1] if local_part else matrix, link_axis, perm=by...  10.3 us
    ppermute x3, starting transfers between devices, detail_ratios(): lax.ppermute(u1[-1] if u1 else matrix, axis_name=link_axis, perm=pages)  8.86 us
    reshape x1, local copies, waits for them, and re-layouts, copied_route(): incoming.reshape(-1, MODEL_WIDTH)  8.19 us
  transfers between devices with their start and end apart: 12, of which 6 were waited for; matrix products, arithmetic and copies ran while one was open for 20% of the time, Pallas kernels for 0%

profile of v1, /device:TPU:0, one launch (start us, length us, event | category | flops | bytes accessed | tf_op | source)
XLA Modules:
  0.0 346.7 jit_solution(976185975121111466)
XLA Ops:
  10.2 3.0 collective-permute-start.4
  13.8 6.2 %copy.61 = bf16[2880,640]{0,1:T(8,128)(2,1)} copy(bf16[2880,640]{1,0:T(8,128)(2,1)} %param.15) | data formatting | bytes 7372800 | tf_op args[3]
  22.5 5.3 %collective-permute-done.1 = bf16[32,2880]{1,0:T(8,128)(2,1)S(1)} collective-permute-done((bf16[32,2880]{1,0:T(8,128)(2,1)S(1)}, bf16[32,2880]{1,0:T(8,128)(2,1)S(1)}, u32[]{:S(2)}, u32[]{:S(2)}) %collective-permute-start.1) | collective-permute-done | bytes 184352 | tf_op jit(solution)/shard_map/ppermute | solution.py:34
  27.8 3.0 collective-permute-start.5
  30.7 3.3 collective-permute-done.2
  35.5 3.0 collective-permute-start.6
  46.6 3.2 gather_fusion
  49.8 3.7 %convolution_bitcast_fusion = f32[256,1,10,64]{0,3,2,1:T(8,128)S(1)} fusion(bf16[256,2880,1]{1,0,2:T(8,128)(2,1)} %bitcast.150, bf16[10,64,2880]{2,1,0:T(8,128)(2,1)} %bitcast.149), kind=kOutput, calls=%fused_computation.20 | convolution fusion | flops 943718400 | bytes 5816320 | tf_op jit(solution)/shard_map/dot_general | solution.py:182
  54.4 4.5 %collective-permute-start.7 = (bf16[128,1,128]{0,2,1:T(8,128)(2,1)}, bf16[128,1,128]{0,2,1:T(8,128)(2,1)}, u32[]{:S(2)}, u32[]{:S(2)}) collective-permute-start(bf16[128,1,128]{0,2,1:T(8,128)(2,1)} %pad_maximum_fusion.3), channel_id=1, source_target_pairs={{0,8},{8,16},{16,24},{24,32},{32,40},{40,48},{48,56},{56,64},{64,7... | collective-permute-start | bytes 98312 | tf_op jit(solution)/shard_map/ppermute | solution.py:50
  73.1 30.9 %reduce-scatter.2.cloned.1.call-done = bf16[32,2880]{1,0:T(8,128)(2,1)} async-done(((bf16[256,2880]{1,0:T(8,128)(2,1)}), bf16[32,2880]{1,0:T(8,128)(2,1)}) %reduce-scatter.2.cloned.1.call-update) | async-done | bytes 184336 | tf_op jit(solution)/shard_map/reduce_scatter | solution.py:205
  110.6 3.0 broadcast_in_dim.93
  113.6 8.0 %all-to-all-start = ((bf16[128,6,2880]{2,1,0:T(8,128)(2,1)}), bf16[128,6,2880]{2,1,0:T(8,128)(2,1)}, u32[]{:S(2)}, u32[]{:S(2)}) async-start(bf16[128,6,2880]{2,1,0:T(8,128)(2,1)} %bitcast.148), calls=%async_computation.1 | async-start | bytes 12058624 | tf_op jit(solution)/shard_map/all_to_all | solution.py:230
  123.9 70.6 %all-to-all-done = bf16[128,6,2880]{2,1,0:T(8,128)(2,1)} async-done(((bf16[128,6,2880]{2,1,0:T(8,128)(2,1)}), bf16[128,6,2880]{2,1,0:T(8,128)(2,1)}, u32[]{:S(2)}, u32[]{:S(2)}) %all-to-all-start) | async-done | bytes 4423712 | tf_op jit(solution)/shard_map/all_to_all | solution.py:230
  194.6 6.4 %all-to-all-start.2 = ((bf16[16,1,16,1,128]{4,2,3,1,0:T(8,128)(2,1)}), bf16[16,1,16,1,128]{4,2,3,1,0:T(8,128)(2,1)S(1)}, u32[]{:S(2)}, u32[]{:S(2)}) async-start(bf16[16,1,16,1,128]{4,2,3,1,0:T(8,128)(2,1)} %bitcast.49), calls=%async_computation.3 | async-start | bytes 131072 | tf_op jit(solution)/shard_map/all_to_all | solution.py:251
  201.0 8.2 %reshape.878 = bf16[768,2880]{1,0:T(8,128)(2,1)} reshape(bf16[128,6,2880]{2,1,0:T(8,128)(2,1)} %all-to-all-done) | data formatting | bytes 8847360 | tf_op jit(solution)/shard_map/reshape | solution.py:141
  209.1 10.8 %fusion = f32[768,1440]{0,1:T(8,128)S(1)} fusion(bf16[768,2880]{1,0:T(8,128)(2,1)} %reshape.878, bf16[1,2880,1440]{1,2,0:T(8,128)(2,1)} %param.21), kind=kOutput, calls=%fused_computation.6 | convolution fusion | flops 6370099200 | bytes 17141760 | tf_op jit(solution)/shard_map/dot_general | solution.py:127
  220.0 8.1 %convolution_convert_fusion = bf16[768,2880]{0,1:T(8,128)(2,1)} fusion(bf16[1,720,2880]{2,1,0:T(8,128)(2,1)} %param.22, f32[768,1440]{0,1:T(8,128)S(1)} %fusion), kind=kOutput, calls=%fused_computation.8 | convolution fusion | flops 3191685120 | bytes 12994560 | tf_op jit(solution)/shard_map/dot_general | solution.py:133
  228.1 6.5 %copy.73 = bf16[768,2880]{1,0:T(8,128)(2,1)} copy(bf16[768,2880]{0,1:T(8,128)(2,1)} %convolution_convert_fusion) | data formatting | bytes 8847360 | tf_op jit(solution)/shard_map/convert_element_type | solution.py:133
  234.6 7.6 %reshape.879 = bf16[128,6,2880]{2,1,0:T(8,128)(2,1)} reshape(bf16[768,2880]{1,0:T(8,128)(2,1)} %copy.73) | data formatting | bytes 8847360 | tf_op jit(solution)/shard_map/reshape | solution.py:141
  242.2 8.4 %all-to-all-start.1 = ((bf16[128,6,2880]{2,1,0:T(8,128)(2,1)}), bf16[128,6,2880]{2,1,0:T(8,128)(2,1)}, u32[]{:S(2)}, u32[]{:S(2)}) async-start(bf16[128,6,2880]{2,1,0:T(8,128)(2,1)} %reshape.879), calls=%async_computation.2 | async-start | bytes 12058624 | tf_op jit(solution)/shard_map/all_to_all | solution.py:230
  252.4 71.2 %all-to-all-done.1 = bf16[128,6,2880]{2,1,0:T(8,128)(2,1)} async-done(((bf16[128,6,2880]{2,1,0:T(8,128)(2,1)}), bf16[128,6,2880]{2,1,0:T(8,128)(2,1)}, u32[]{:S(2)}, u32[]{:S(2)}) %all-to-all-start.1) | async-done | bytes 4423712 | tf_op jit(solution)/shard_map/all_to_all | solution.py:230
  323.6 6.0 %convert_reduce_fusion = f32[32,6,2880]{2,1,0:T(8,128)} fusion(bf16[128,6,2880]{2,1,0:T(8,128)(2,1)} %all-to-all-done.1), kind=kLoop, calls=%fused_computation.5 | loop fusion | flops 3870720 | bytes 6635520 | tf_op jit(solution)/shard_map/reduce_sum | solution.py:145
  333.8 2.9 reshape.905
  336.7 2.4 multiply_reduce_fusion
  (152 shorter events, 46.1 us)
Async XLA Ops:
  7.2 63.0 %copy-start = (bf16[512,2880]{0,1:T(8,128)(2,1)S(1)}, bf16[512,2880]{0,1:T(8,128)(2,1)}, u32[]{:S(2)}) copy-start(bf16[512,2880]{0,1:T(8,128)(2,1)} %param.17) | copy-start | bytes 8847364
  7.2 96.9 %reduce-scatter.2.cloned.1.call-start = ((), (), s32[]{:S(2)}) async-start(), calls=%async_computation.4 | async-start | bytes 1695744 | tf_op jit(solution)/shard_map/reduce_scatter | solution.py:205
  10.2 11.3 %collective-permute-start = (bf16[32,2880]{1,0:T(8,128)(2,1)}, bf16[32,2880]{1,0:T(8,128)(2,1)S(1)}, u32[]{:S(2)}, u32[]{:S(2)}) collective-permute-start(bf16[32,2880]{1,0:T(8,128)(2,1)} %fusion.15), channel_id=1, source_target_pairs={{0,1},{1,2},{2,3},{3,4},{4,5},{5,6},{6,7},{7,0},{8,9},{9,10},{10,1... | collective-permute-start | bytes 552968 | tf_op jit(solution)/shard_map/ppermute | solution.py:34
  10.2 17.6 %collective-permute-start.4 = (bf16[32,2880]{1,0:T(8,128)(2,1)}, bf16[32,2880]{1,0:T(8,128)(2,1)S(1)}, u32[]{:S(2)}, u32[]{:S(2)}) collective-permute-start(bf16[32,2880]{1,0:T(8,128)(2,1)} %fusion.15), channel_id=1, source_target_pairs={{1,0},{2,1},{3,2},{4,3},{5,4},{6,5},{7,6},{0,7},{9,8},{10,9},{11,1... | collective-permute-start | bytes 552968 | tf_op jit(solution)/shard_map/ppermute | solution.py:37
  13.8 6.2 %copy-start.17 = (s32[4]{0:T(128)S(1)}, s32[4]{0:T(128)}, u32[]{:S(2)}) copy-start(s32[4]{0:T(128)} %param.13) | copy-start | bytes 52
  13.8 7.1 %copy-start.18 = (f32[8]{0:T(128)S(1)}, f32[8]{0:T(128)}, u32[]{:S(2)}) copy-start(f32[8]{0:T(128)} %param.16) | copy-start | bytes 100
  13.8 29.1 %copy-start.2 = (bf16[32,2880]{1,0:T(8,128)(2,1)S(1)}, bf16[32,2880]{1,0:T(8,128)(2,1)}, u32[]{:S(2)}) copy-start(bf16[32,2880]{1,0:T(8,128)(2,1)} %param.12) | copy-start | bytes 552964
  21.5 6.2 %collective-permute-start.1 = (bf16[32,2880]{1,0:T(8,128)(2,1)S(1)}, bf16[32,2880]{1,0:T(8,128)(2,1)S(1)}, u32[]{:S(2)}, u32[]{:S(2)}) collective-permute-start(bf16[32,2880]{1,0:T(8,128)(2,1)S(1)} %collective-permute-done), channel_id=1, source_target_pairs={{0,1},{1,2},{2,3},{3,4},{4,5},{5,6},{6,7},{7,0},{8,9},{9,10},{10,1... | collective-permute-start | bytes 552968 | tf_op jit(solution)/shard_map/ppermute | solution.py:34
  27.8 6.2 %collective-permute-start.2 = (bf16[32,2880]{1,0:T(8,128)(2,1)S(1)}, bf16[32,2880]{1,0:T(8,128)(2,1)S(1)}, u32[]{:S(2)}, u32[]{:S(2)}) collective-permute-start(bf16[32,2880]{1,0:T(8,128)(2,1)S(1)} %collective-permute-done.1), channel_id=1, source_target_pairs={{0,1},{1,2},{2,3},{3,4},{4,5},{5,6},{6,7},{7,0},{8,9},{9,10},{10,1... | collective-permute-start | bytes 552968 | tf_op jit(solution)/shard_map/ppermute | solution.py:34
  27.8 7.7 %collective-permute-start.5 = (bf16[32,2880]{1,0:T(8,128)(2,1)S(1)}, bf16[32,2880]{1,0:T(8,128)(2,1)S(1)}, u32[]{:S(2)}, u32[]{:S(2)}) collective-permute-start(bf16[32,2880]{1,0:T(8,128)(2,1)S(1)} %collective-permute-done.4), channel_id=1, source_target_pairs={{1,0},{2,1},{3,2},{4,3},{5,4},{6,5},{7,6},{0,7},{9,8},{10,9},{11,1... | collective-permute-start | bytes 552968 | tf_op jit(solution)/shard_map/ppermute | solution.py:37
  34.0 6.2 %collective-permute-start.3 = (bf16[32,2880]{1,0:T(8,128)(2,1)S(1)}, bf16[32,2880]{1,0:T(8,128)(2,1)S(1)}, u32[]{:S(2)}, u32[]{:S(2)}) collective-permute-start(bf16[32,2880]{1,0:T(8,128)(2,1)S(1)} %collective-permute-done.2), channel_id=1, source_target_pairs={{0,1},{1,2},{2,3},{3,4},{4,5},{5,6},{6,7},{7,0},{8,9},{9,10},{10,1... | collective-permute-start | bytes 552968 | tf_op jit(solution)/shard_map/ppermute | solution.py:34
  35.5 10.4 %collective-permute-start.6 = (bf16[32,2880]{1,0:T(8,128)(2,1)S(1)}, bf16[32,2880]{1,0:T(8,128)(2,1)S(1)}, u32[]{:S(2)}, u32[]{:S(2)}) collective-permute-start(bf16[32,2880]{1,0:T(8,128)(2,1)S(1)} %collective-permute-done.5), channel_id=1, source_target_pairs={{1,0},{2,1},{3,2},{4,3},{5,4},{6,5},{7,6},{0,7},{9,8},{10,9},{11,1... | collective-permute-start | bytes 552968 | tf_op jit(solution)/shard_map/ppermute | solution.py:37
  49.8 9.1 %copy-start.6 = (f32[256,32]{0,1:T(8,128)S(1)}, f32[256,32]{0,1:T(8,128)}, u32[]{:S(2)}) copy-start(f32[256,32]{0,1:T(8,128)} %get-tuple-element.13) | copy-start | bytes 98308
  54.4 11.8 %collective-permute-start.7 = (bf16[128,1,128]{0,2,1:T(8,128)(2,1)}, bf16[128,1,128]{0,2,1:T(8,128)(2,1)}, u32[]{:S(2)}, u32[]{:S(2)}) collective-permute-start(bf16[128,1,128]{0,2,1:T(8,128)(2,1)} %pad_maximum_fusion.3), channel_id=1, source_target_pairs={{0,8},{8,16},{16,24},{24,32},{32,40},{40,48},{48,56},{56,64},{64,7... | collective-permute-start | bytes 98312 | tf_op jit(solution)/shard_map/ppermute | solution.py:50
  60.9 6.1 %copy-start.7 = (bf16[2,128,1,64]{1,3,0,2:T(8,128)(2,1)S(1)}, bf16[2,128,1,64]{1,3,0,2:T(8,128)(2,1)}, u32[]{:S(2)}) copy-start(bf16[2,128,1,64]{1,3,0,2:T(8,128)(2,1)} %copy.65) | copy-start | bytes 98308
  72.4 32.8 %copy-start.9 = (f32[2880]{0:T(1024)S(1)}, f32[2880]{0:T(1024)}, u32[]{:S(2)}) copy-start(f32[2880]{0:T(1024)} %param.18) | copy-start | bytes 34564
  113.6 8.0 %copy-start.10 = (s32[256]{0:T(256)S(1)}, s32[256]{0:T(256)}, u32[]{:S(2)}) copy-start(s32[256]{0:T(256)} %param.23) | copy-start | bytes 3076
  113.6 81.0 %all-to-all-start = ((bf16[128,6,2880]{2,1,0:T(8,128)(2,1)}), bf16[128,6,2880]{2,1,0:T(8,128)(2,1)}, u32[]{:S(2)}, u32[]{:S(2)}) async-start(bf16[128,6,2880]{2,1,0:T(8,128)(2,1)} %bitcast.148), calls=%async_computation.1 | async-start | bytes 12058624 | tf_op jit(solution)/shard_map/all_to_all | solution.py:230
  194.6 47.6 %all-to-all-start.2 = ((bf16[16,1,16,1,128]{4,2,3,1,0:T(8,128)(2,1)}), bf16[16,1,16,1,128]{4,2,3,1,0:T(8,128)(2,1)S(1)}, u32[]{:S(2)}, u32[]{:S(2)}) async-start(bf16[16,1,16,1,128]{4,2,3,1,0:T(8,128)(2,1)} %bitcast.49), calls=%async_computation.3 | async-start | bytes 131072 | tf_op jit(solution)/shard_map/all_to_all | solution.py:251
  242.2 8.9 %copy-start.15 = (f32[32,4]{0,1:T(4,128)S(1)}, f32[32,4]{0,1:T(4,128)}, u32[]{:S(2)}) copy-start(f32[32,4]{0,1:T(4,128)} %param.20) | copy-start | bytes 1540
  242.2 81.4 %all-to-all-start.1 = ((bf16[128,6,2880]{2,1,0:T(8,128)(2,1)}), bf16[128,6,2880]{2,1,0:T(8,128)(2,1)}, u32[]{:S(2)}, u32[]{:S(2)}) async-start(bf16[128,6,2880]{2,1,0:T(8,128)(2,1)} %reshape.879), calls=%async_computation.2 | async-start | bytes 12058624 | tf_op jit(solution)/shard_map/all_to_all | solution.py:230
  252.4 77.2 %copy-start.5 = (bf16[16,16,128]{2,1,0:T(8,128)(2,1)}, bf16[16,16,128]{2,1,0:T(8,128)(2,1)S(1)}, u32[]{:S(2)}) copy-start(bf16[16,16,128]{2,1,0:T(8,128)(2,1)S(1)} %scatter_fusion) | copy-start | bytes 196612
  333.8 5.3 %copy-start.3 = (bf16[32,2880]{1,0:T(8,128)(2,1)S(1)}, bf16[32,2880]{1,0:T(8,128)(2,1)}, u32[]{:S(2)}) copy-start(bf16[32,2880]{1,0:T(8,128)(2,1)} %reduce-scatter.2.cloned.1.call-done) | copy-start | bytes 552964
  333.8 6.1 %copy-start.1 = (bf16[512,2880]{0,1:T(8,128)(2,1)S(1)}, bf16[512,2880]{0,1:T(8,128)(2,1)}, u32[]{:S(2)}) copy-start(bf16[512,2880]{0,1:T(8,128)(2,1)} %param.17) | copy-start | bytes 8847364
  (7 other events, 19.6 us)
Sparse Core Ops, SparseCore 0:
  72.5 31.5 reduce-scatter.1
